TPU v7x, 32 devices: a whole 2x2x4 slice. The times are simulated.
32 devices in a mesh: dp: 8 (over y, x, core), tensor: 4 (over z).
Axes of the slice: x: 2, y: 2, z: 4, core: 2. Of those that a mesh axis runs over, the one named last changes fastest.
Arguments:
- tokens_in: bfloat16 [32, 577, 1024], P('dp'), may hold values from -6 to 6
- norm1_gain: float32 [1024], replicated, may hold values from 0.5 to 1.5
- norm1_bias: float32 [1024], replicated, may hold values from -3 to 3
- w_qkv: bfloat16 [1024, 3, 16, 64], P(None, None, 'tensor'), may hold values from -0.1875 to 0.1875
- bias_qv: float32 [2, 16, 64], P(None, 'tensor'), may hold values from -3 to 3
- w_out: bfloat16 [16, 64, 1024], P('tensor'), may hold values from -0.75 to 0.75
- bias_out: float32 [1024], replicated, may hold values from -3 to 3
- norm2_gain: float32 [1024], replicated, may hold values from 0.5 to 1.5
- norm2_bias: float32 [1024], replicated, may hold values from -3 to 3
- w_up: bfloat16 [1024, 4096], P(None, 'tensor'), may hold values from -0.1875 to 0.1875
- bias_up: float32 [4096], P('tensor'), may hold values from -3 to 3
- w_down: bfloat16 [4096, 1024], P('tensor'), may hold values from -0.09375 to 0.09375
- bias_down: float32 [1024], replicated, may hold values from -3 to 3
- cotangent: bfloat16 [32, 577, 1024], P('dp'), may hold values from -6 to 6
Outputs:
- block_out: bfloat16 [32, 577, 1024], P('dp')
- grad_input: float32 [32, 577, 1024], P('dp')
- grad_norm1_gain: float32 [1024], replicated
- grad_norm1_bias: float32 [1024], replicated
- grad_w_qkv: float32 [1024, 3, 16, 64], P(None, None, 'tensor')
- grad_bias_qv: float32 [2, 16, 64], P(None, 'tensor')
- grad_w_out: float32 [16, 64, 1024], P('tensor')
- grad_bias_out: float32 [1024], replicated
- grad_norm2_gain: float32 [1024], replicated
- grad_norm2_bias: float32 [1024], replicated
- grad_w_up: float32 [1024, 4096], P(None, 'tensor')
- grad_bias_up: float32 [4096], P('tensor')
- grad_w_down: float32 [4096, 1024], P('tensor')
- grad_bias_down: float32 [1024], replicated
All inputs are finite; a program needn't handle non-finite values.
Results may differ from a plain program's by a relative error of at most 0.024.
Values may be sent and summed in bfloat16 or wider, within the bound.
No kernel may reach another device: no remote copies, remote signals or barrier semaphores. Data moves between devices by JAX's collectives and lax.ppermute only.
A program may use at most 256 MiB of HBM per device.

v0:
```python
import jax
import jax.numpy as jnp
from jax import lax
from jax.sharding import PartitionSpec as P

inv_root2 = 0.7071067811865476
inv_root_2pi = 0.3989422804014327


def layer_norm(values, gain, shift):
    centre = jnp.mean(values, axis=-1, keepdims=True)
    centred = values - centre
    spread = jnp.mean(centred * centred, axis=-1, keepdims=True)
    inv_std = lax.rsqrt(spread + 1e-06)
    whitened = centred * inv_std
    return (whitened, inv_std, whitened * gain + shift)


def norm_back(grad_out, whitened, inv_std, gain):
    grad_white = grad_out * gain
    inner_part = (
        grad_white
        - jnp.mean(grad_white, axis=-1, keepdims=True)
        - whitened * jnp.mean(grad_white * whitened, axis=-1, keepdims=True)
    )
    return (inv_std * inner_part, jnp.sum(grad_out * whitened, axis=0), jnp.sum(grad_out, axis=0))


def gelu(pre_act):
    return 0.5 * pre_act * (1.0 + lax.erf(pre_act * inv_root2))


def gelu_slope(pre_act):
    return 0.5 * (1.0 + lax.erf(pre_act * inv_root2)) + pre_act * inv_root_2pi * jnp.exp(
        -0.5 * pre_act * pre_act
    )


def attend(queries, key_rows, values, score_scale):
    scores = (
        jnp.einsum("qhd,khd->hqk", queries, key_rows, preferred_element_type=jnp.float32)
        * score_scale
    )
    row_max = jnp.max(scores, axis=-1, keepdims=True)
    expos = jnp.exp(scores - row_max)
    expsum = jnp.sum(expos, axis=-1, keepdims=True)
    probs = (expos / expsum).astype(jnp.bfloat16)
    attended = jnp.einsum("hqk,khd->qhd", probs, values, preferred_element_type=jnp.float32).astype(
        jnp.bfloat16
    )
    return (attended, (row_max + jnp.log(expsum))[..., 0])


def attend_back(queries, key_rows, values, upstream, log_norm, score_scale):
    scores = (
        jnp.einsum("qhd,khd->hqk", queries, key_rows, preferred_element_type=jnp.float32)
        * score_scale
    )
    probs = jnp.exp(scores - log_norm[..., None])
    grad_values = jnp.einsum(
        "hqk,qhd->khd", probs.astype(jnp.bfloat16), upstream, preferred_element_type=jnp.float32
    )
    grad_prob = jnp.einsum("qhd,khd->hqk", upstream, values, preferred_element_type=jnp.float32)
    row_delta = jnp.sum(probs * grad_prob, axis=-1, keepdims=True)
    grad_score = (probs * (grad_prob - row_delta) * score_scale).astype(jnp.bfloat16)
    grad_queries = jnp.einsum(
        "hqk,khd->qhd", grad_score, key_rows, preferred_element_type=jnp.float32
    )
    grad_keys = jnp.einsum("hqk,qhd->khd", grad_score, queries, preferred_element_type=jnp.float32)
    return (grad_queries, grad_keys, grad_values)


def body(
    tokens_in,
    norm1_gain,
    norm1_bias,
    w_qkv,
    bias_qv,
    w_out,
    bias_out,
    norm2_gain,
    norm2_bias,
    w_up,
    bias_up,
    w_down,
    bias_down,
    cotangent,
):
    images, seq_len, model_width = tokens_in.shape
    tok_rows = images * seq_len
    heads_local = w_qkv.shape[2]
    head_size = w_qkv.shape[3]
    inner_width = heads_local * head_size
    score_scale = head_size ** (-0.5)
    image_shape = (images, seq_len, heads_local, head_size)
    x_float = tokens_in.reshape(tok_rows, model_width).astype(jnp.float32)
    white1, inv1, normed1 = layer_norm(x_float, norm1_gain, norm1_bias)
    first_in = normed1.astype(jnp.bfloat16)
    w_flat = w_qkv.reshape(model_width, 3 * inner_width)
    projected = jnp.dot(first_in, w_flat, preferred_element_type=jnp.float32).reshape(
        tok_rows, 3, heads_local, head_size
    )
    queries = (projected[:, 0] + bias_qv[0]).astype(jnp.bfloat16).reshape(image_shape)
    key_rows = projected[:, 1].astype(jnp.bfloat16).reshape(image_shape)
    values = (projected[:, 2] + bias_qv[1]).astype(jnp.bfloat16).reshape(image_shape)
    attended, log_norm = lax.map(
        lambda packed: attend(packed[0], packed[1], packed[2], score_scale),
        (queries, key_rows, values),
    )
    head_flat = attended.reshape(tok_rows, inner_width)
    out_rows = w_out.reshape(inner_width, model_width)
    attn_sum = lax.psum(
        jnp.dot(head_flat, out_rows, preferred_element_type=jnp.float32).astype(jnp.bfloat16),
        "tensor",
    ).astype(jnp.float32)
    hidden1 = x_float + attn_sum + bias_out
    white2, inv2, normed2 = layer_norm(hidden1, norm2_gain, norm2_bias)
    second_in = normed2.astype(jnp.bfloat16)
    pre_act = jnp.dot(second_in, w_up, preferred_element_type=jnp.float32) + bias_up
    hidden_act = gelu(pre_act).astype(jnp.bfloat16)
    mlp_sum = lax.psum(
        jnp.dot(hidden_act, w_down, preferred_element_type=jnp.float32).astype(jnp.bfloat16),
        "tensor",
    ).astype(jnp.float32)
    block_out = (hidden1 + mlp_sum + bias_down).astype(jnp.bfloat16)
    grad_out = cotangent.reshape(tok_rows, model_width)
    grad_float = grad_out.astype(jnp.float32)
    grad_bias_down = jnp.sum(grad_float, axis=0)
    grad_w_down = jnp.einsum("rf,re->fe", hidden_act, grad_out, preferred_element_type=jnp.float32)
    grad_hidden = jnp.einsum("re,fe->rf", grad_out, w_down, preferred_element_type=jnp.float32)
    grad_pre = grad_hidden * gelu_slope(pre_act)
    grad_bias_up = jnp.sum(grad_pre, axis=0)
    grad_pre_bf = grad_pre.astype(jnp.bfloat16)
    grad_w_up = jnp.einsum("re,rf->ef", second_in, grad_pre_bf, preferred_element_type=jnp.float32)
    grad_second = lax.psum(
        jnp.einsum("rf,ef->re", grad_pre_bf, w_up, preferred_element_type=jnp.float32).astype(
            jnp.bfloat16
        ),
        "tensor",
    ).astype(jnp.float32)
    grad_norm2_in, grad_norm2_gain, grad_norm2_bias = norm_back(
        grad_second, white2, inv2, norm2_gain
    )
    grad_hidden1 = grad_float + grad_norm2_in
    grad_bias_out = jnp.sum(grad_hidden1, axis=0)
    grad_h1_bf = grad_hidden1.astype(jnp.bfloat16)
    grad_w_out = jnp.einsum(
        "rk,re->ke", head_flat, grad_h1_bf, preferred_element_type=jnp.float32
    ).reshape(heads_local, head_size, model_width)
    upstream = jnp.einsum(
        "re,ke->rk", grad_h1_bf, out_rows, preferred_element_type=jnp.float32
    ).astype(jnp.bfloat16)
    grad_queries, grad_keys, grad_values = lax.map(
        lambda packed: attend_back(
            packed[0], packed[1], packed[2], packed[3], packed[4], score_scale
        ),
        (queries, key_rows, values, upstream.reshape(image_shape), log_norm),
    )
    grad_queries = grad_queries.reshape(tok_rows, heads_local, head_size)
    grad_keys = grad_keys.reshape(tok_rows, heads_local, head_size)
    grad_values = grad_values.reshape(tok_rows, heads_local, head_size)
    grad_bias_qv = jnp.stack([jnp.sum(grad_queries, axis=0), jnp.sum(grad_values, axis=0)])
    grad_qkv = (
        jnp.stack([grad_queries, grad_keys, grad_values], axis=1)
        .astype(jnp.bfloat16)
        .reshape(tok_rows, 3 * inner_width)
    )
    grad_w_qkv = jnp.einsum(
        "re,rk->ek", first_in, grad_qkv, preferred_element_type=jnp.float32
    ).reshape(model_width, 3, heads_local, head_size)
    grad_first = lax.psum(
        jnp.einsum("rk,ek->re", grad_qkv, w_flat, preferred_element_type=jnp.float32).astype(
            jnp.bfloat16
        ),
        "tensor",
    ).astype(jnp.float32)
    grad_norm1_in, grad_norm1_gain, grad_norm1_bias = norm_back(
        grad_first, white1, inv1, norm1_gain
    )
    grad_input = (grad_hidden1 + grad_norm1_in).reshape(images, seq_len, model_width)
    everything = (
        lax.psum(grad_norm1_gain.astype(jnp.bfloat16), "dp").astype(jnp.float32),
        lax.psum(grad_norm1_bias.astype(jnp.bfloat16), "dp").astype(jnp.float32),
        lax.psum(grad_w_qkv.astype(jnp.bfloat16), "dp").astype(jnp.float32),
        lax.psum(grad_bias_qv.astype(jnp.bfloat16), "dp").astype(jnp.float32),
        lax.psum(grad_w_out.astype(jnp.bfloat16), "dp").astype(jnp.float32),
        lax.psum(grad_bias_out.astype(jnp.bfloat16), "dp").astype(jnp.float32),
        lax.psum(grad_norm2_gain.astype(jnp.bfloat16), "dp").astype(jnp.float32),
        lax.psum(grad_norm2_bias.astype(jnp.bfloat16), "dp").astype(jnp.float32),
        lax.psum(grad_w_up.astype(jnp.bfloat16), "dp").astype(jnp.float32),
        lax.psum(grad_bias_up.astype(jnp.bfloat16), "dp").astype(jnp.float32),
        lax.psum(grad_w_down.astype(jnp.bfloat16), "dp").astype(jnp.float32),
        lax.psum(grad_bias_down.astype(jnp.bfloat16), "dp").astype(jnp.float32),
    )
    return (
        block_out.reshape(images, seq_len, model_width),
        grad_input,
        everything[0],
        everything[1],
        everything[2],
        everything[3],
        everything[4],
        everything[5],
        everything[6],
        everything[7],
        everything[8],
        everything[9],
        everything[10],
        everything[11],
    )


def solution(mesh):
    placed = (
        P("dp", None, None),
        P(),
        P(),
        P(None, None, "tensor", None),
        P(None, "tensor", None),
        P("tensor", None, None),
        P(),
        P(),
        P(),
        P(None, "tensor"),
        P("tensor"),
        P("tensor", None),
        P(),
        P("dp", None, None),
    )
    return jax.shard_map(
        body,
        mesh=mesh,
        in_specs=placed,
        out_specs=(
            P("dp", None, None),
            P("dp", None, None),
            P(),
            P(),
            P(None, None, "tensor", None),
            P(None, "tensor", None),
            P("tensor", None, None),
            P(),
            P(),
            P(),
            P(None, "tensor"),
            P("tensor"),
            P("tensor", None),
            P(),
        ),
        check_vma=False,
    )
```

profile of v0, /device:TPU:0, one launch (start us, length us, event | category | flops | bytes accessed | tf_op | source)
XLA Modules:
  0.0 1275.7 jit_solution(7778896030707905259)
XLA Ops:
  57.4 25.5 %while.26 = (s32[]{:T(128)}, bf16[4,577,4,64]{1,3,2,0:T(8,128)(2,1)}, f32[4,4,577]{2,1,0:T(4,128)S(1)}, bf16[4,577,4,64]{1,3,2,0:T(8,128)(2,1)}, bf16[4,577,4,64...) while((s32[]{:T(128)}, bf16[4,577,4,64]{1,3,2,0:T(8,128)(2,1)}, ...), condition=%wide.region_5.6_spmd, body=%wide.region_2.5_spmd.sunk | while | flops 353050112 | bytes 17370328 | solution.py:106
  124.2 146.8 %all-reduce.8.cloned.1.call-done = bf16[2308,1024]{1,0:T(8,128)(2,1)} async-done(((bf16[2308,1024]{1,0:T(8,128)(2,1)}), bf16[2308,1024]{1,0:T(8,128)(2,1)}) %all-reduce.8.cloned.1.call-update) | async-done | bytes 4726800 | tf_op jit(solution)/shard_map/psum | solution.py:112
  270.9 9.9 fusion.129
  297.0 11.2 fusion.131
  317.3 10.2 convolution_convert_fusion.4
  335.6 153.3 %all-reduce.10.cloned.1.call-done = bf16[2308,1024]{1,0:T(8,128)(2,1)} async-done(((bf16[2308,1024]{1,0:T(8,128)(2,1)}), bf16[2308,1024]{1,0:T(8,128)(2,1)}) %all-reduce.10.cloned.1.call-update) | async-done | bytes 4726800 | tf_op jit(solution)/shard_map/psum | solution.py:135
  517.4 198.5 %while.27 = (s32[]{:T(128)}, f32[4,577,4,64]{1,3,2,0:T(8,128)}, bf16[4,577,4,64]{1,0,3,2:T(4,128)(2,1)}, f32[4,577,4,64]{1,3,2,0:T(8,128)}, bf16[4,577,4,64]{1,3...) while((s32[]{:T(128)}, f32[4,577,4,64]{1,3,2,0:T(8,128)}, ...), condition=%wide.region_15.16_spmd, body=%wide.region_13.15_spmd.sunk | while | flops 880270016 | bytes 90938144 | solution.py:153
  528.8 11.9 fusion.181
  540.7 12.2 fusion.180
  554.4 12.7 dynamic_update_slice.31
  578.4 11.9 fusion.181
  590.3 12.2 fusion.180
  604.0 12.7 dynamic_update_slice.31
  628.0 11.9 fusion.181
  639.9 12.2 fusion.180
  653.6 12.7 dynamic_update_slice.31
  677.6 11.9 fusion.181
  689.5 12.2 fusion.180
  703.2 12.7 dynamic_update_slice.31
  766.1 74.9 %all-reduce.12.cloned.1.call-done = (bf16[1024,3,4,64]{0,3,2,1:T(8,128)(2,1)}, bf16[4,64,1024]{2,1,0:T(8,128)(2,1)}, bf16[1024,1024]{1,0:T(8,128)(2,1)}, bf16[1024,1024]{1,0:T(8,128)(2,1)}) async-done(((bf16[1024,3,4,64]{0,3,2,1:T(8,128)(2,1)}, bf16[4,64,1024]{2,1,0:T(8,128)(2,1)}, bf16[1024,1024]{1,0:T(8,128)(2,1)}, bf16[1024,1024]{1,0:T(8,128)(2,1)}), (bf16[1024,3,4,64]{0,3,2,1:T(8,128)(2,1)}, ...) | async-done | bytes 6291472 | tf_op jit(solution)/shard_map/psum | solution.py:184
  851.7 318.5 %all-reduce.14.cloned.1.call-done = (bf16[2308,1024]{1,0:T(8,128)(2,1)}, bf16[2308,1024]{1,0:T(8,128)(2,1)}) async-done(((bf16[2308,1024]{1,0:T(8,128)(2,1)}, bf16[2308,1024]{1,0:T(8,128)(2,1)}), (bf16[2308,1024]{1,0:T(8,128)(2,1)}, bf16[2308,1024]{1,0:T(8,128)(2,1)})) %all-reduce.14.cloned.1.call-update) | async-done | bytes 9453584 | tf_op jit(solution)/shard_map/psum | solution.py:121
  1182.0 23.8 %all-reduce = (bf16[1024]{0:T(1024)(128)(2,1)S(1)}, bf16[1024]{0:T(1024)(128)(2,1)S(1)}, bf16[2,4,64]{2,1,0:T(4,128)(2,1)S(1)}, bf16[1024]{0:T(1024)(128)(2,1)S(...) all-reduce(bf16[1024]{0:T(1024)(128)(2,1)S(1)} %get-tuple-element.2, ...), channel_id=1, replica_groups=mesh['dp'=8,'tensor'=4] {'dp'}, use_global_device_ids=true, to_apply=%region_20.21 | all-reduce | flops 7680 | bytes 30720 | tf_op jit(solution)/shard_map/psum | solution.py:182
  1233.6 13.2 %fusion.94 = f32[2308,1024]{1,0:T(8,128)} fusion(f32[2308,1024]{1,0:T(8,128)} %copy-done.4, bf16[2308,1024]{1,0:T(8,128)(2,1)} %get-tuple-element.266, f32[2308,1024]{1,0:T(8,128)} %reshape.210, f32[2308]{0:T(1024)S(1)} %broadcast_multiply_fusion.1, f32[2308]{0:T(1024)S(1)} %div.41, f32[2308]{0:T(1024)S(1)} %broadcast_multiply_fusion.2, ...), kind=kLoop, calls=%fused_computation.84 | loop fusion | flops 21270528 | bytes 33128512 | tf_op jit(solution)/shard_map/add | solution.py:180
  1255.4 13.5 %copy.108 = f32[4,577,1024]{2,0,1:T(4,128)} copy(f32[4,577,1024]{2,1,0:T(8,128)} %reshape.209) | data formatting | bytes 18907136
  (209 shorter events, 338.3 us)
Async XLA Ops:
  7.2 278.7 %copy-start = (bf16[1024,1024]{1,0:T(8,128)(2,1)S(1)}, bf16[1024,1024]{1,0:T(8,128)(2,1)}, u32[]{:S(2)}) copy-start(bf16[1024,1024]{1,0:T(8,128)(2,1)} %param.27) | copy-start | bytes 6291460
  7.2 8.7 copy-start.19
  7.2 8.7 copy-start.23
  7.2 263.7 %all-reduce.8.cloned.1.call-start = ((), (), s32[]{:S(2)}) async-start(), calls=%async_computation | async-start | bytes 9469952 | tf_op jit(solution)/shard_map/psum | solution.py:112
  82.9 12.5 copy-start.7
  95.4 393.6 %all-reduce.10.cloned.1.call-start = ((), (), s32[]{:S(2)}) async-start(), calls=%async_computation.1 | async-start | bytes 9469952 | tf_op jit(solution)/shard_map/psum | solution.py:135
  115.7 155.2 %copy-start.24 = (f32[1024]{0:T(1024)S(1)}, f32[1024]{0:T(1024)}, u32[]{:S(2)}) copy-start(f32[1024]{0:T(1024)} %param.24) | copy-start | bytes 12292
  280.9 16.1 %slice-start.3 = ((s8[4734976]{0:T(1024)(128)(4,1)}), s8[4194304]{0:T(1024)(128)(4,1)S(1)}, s32[]{:S(2)}) async-start(s8[4734976]{0:T(1024)(128)(4,1)} %bitcast.172), calls=%async_computation.7 | async-start | bytes 8388608
  287.3 9.7 slice-start.4
  287.3 9.7 copy-start.28
  317.2 10.3 slice-start
  317.2 523.8 %all-reduce.12.cloned.1.call-start = ((), (), s32[]{:S(2)}) async-start(), calls=%async_computation.2 | async-start | bytes 12582912 | tf_op jit(solution)/shard_map/psum | solution.py:184
  317.3 10.2 slice-start.1
  317.3 10.2 slice-start.2
  317.3 10.2 copy-start.33
  489.0 9.1 copy-start.6
  737.9 9.8 copy-start.17
  737.9 432.4 %all-reduce.14.cloned.1.call-start = ((), (), s32[]{:S(2)}) async-start(), calls=%async_computation.3 | async-start | bytes 18939904 | tf_op jit(solution)/shard_map/psum | solution.py:121
  737.9 9.7 copy-start.18
  737.9 9.7 copy-start.29
  849.2 324.1 %copy-start.20 = (f32[1024]{0:T(1024)S(1)}, f32[1024]{0:T(1024)}, u32[]{:S(2)}) copy-start(f32[1024]{0:T(1024)} %param.19) | copy-start | bytes 12292
  1173.3 8.6 copy-start.22
  1173.4 37.2 %copy-start.26 = (f32[1024]{0:T(1024)S(1)}, f32[1024]{0:T(1024)}, u32[]{:S(2)}) copy-start(f32[1024]{0:T(1024)} %param.30) | copy-start | bytes 12292
  1246.8 22.1 %copy-start.1 = (bf16[1024,1024]{1,0:T(8,128)(2,1)S(1)}, bf16[1024,1024]{1,0:T(8,128)(2,1)}, u32[]{:S(2)}) copy-start(bf16[1024,1024]{1,0:T(8,128)(2,1)} %param.27) | copy-start | bytes 6291460
  (22 other events, 100.7 us)
Sparse Core Ops, SparseCore 0:
  95.5 175.3 all-reduce.7
  317.3 171.6 all-reduce.9
  738.0 102.9 all-reduce.11
  844.0 326.1 all-reduce.13
where the time goes:
time: 1290 us; the launch traced here: 1280 us
  waiting for transfers between devices  694 us (54%)
  matrix products  238 us (18%)
  local copies, waits for them, and re-layouts  192 us (15%)
  other arithmetic  113 us (9%)
  blocking collectives  23.8 us (2%)
  between operations  14.5 us (1%)
    psum x1, waiting for transfers between devices, body(): lax.psum(jnp.dot(hidden_act, w_down, preferred_element_type=jnp.float32)....  319 us
    psum x1, waiting for transfers between devices, body(): lax.psum(jnp.einsum('rf,ef->re', grad_pre_bf, w_up, preferred_element_typ...  153 us
    psum x1, waiting for transfers between devices, body(): lax.psum(jnp.dot(head_flat, out_rows, preferred_element_type=jnp.float32)...  147 us
    psum x1, waiting for transfers between devices, body(): lax.psum(grad_w_qkv.astype(jnp.bfloat16), 'dp').astype(jnp.float32)  74.9 us
    dynamic_update_slice x8, local copies, waits for them, and re-layouts, body(): lax.map(lambda packed: attend_back(packed[0], packed[1], packed[2], packe...  56.6 us
    dot_general x4, matrix products, attend_back(): jnp.einsum('hqk,khd->qhd', grad_score, key_rows, preferred_element_type=j...  48.8 us
    dot_general x4, matrix products, attend_back(): jnp.einsum('hqk,qhd->khd', grad_score, queries, preferred_element_type=jn...  47.7 us
    unnamed x81, local copies, waits for them, and re-layouts  36.1 us
  transfers between devices with their start and end apart: 4, of which 4 were waited for; matrix products, arithmetic and copies ran while one was open for 7% of the time, Pallas kernels for 0%

commit v1 on v0

--- a/solution.py
+++ b/solution.py
@@ -5,6 +5,11 @@
 
 inv_root2 = 0.7071067811865476
 inv_root_2pi = 0.3989422804014327
+
+
+def summed_here(x, axis):
+    parts = lax.all_gather(x, axis)
+    return jnp.sum(parts, axis=0)
 
 
 def layer_norm(values, gain, shift):
@@ -132,7 +137,7 @@
     grad_bias_up = jnp.sum(grad_pre, axis=0)
     grad_pre_bf = grad_pre.astype(jnp.bfloat16)
     grad_w_up = jnp.einsum("re,rf->ef", second_in, grad_pre_bf, preferred_element_type=jnp.float32)
-    grad_second = lax.psum(
+    grad_second = summed_here(
         jnp.einsum("rf,ef->re", grad_pre_bf, w_up, preferred_element_type=jnp.float32).astype(
             jnp.bfloat16
         ),

time: 1290 us -> 1450 us (1.12)
  waiting for transfers between devices: 694 us -> 848 us
  other arithmetic: 113 us -> 128 us
    all_gather x0 -> x1, waiting for transfers between devices: none -> 304 us  [summed_here(): parts = lax.all_gather(x, axis)]
    psum x1 -> x0, waiting for transfers between devices: 153 us -> none  [body(): lax.psum(jnp.einsum('rf,ef->re', grad_pre_bf, w_up, preferred_element_typ...]
    reduce_sum x2, other arithmetic: 6.22 us -> 21.5 us  [norm_back(): jnp.sum(grad_out, axis=0)]
    unnamed x81 -> x83, local copies, waits for them, and re-layouts: 36.1 us -> 35.8 us
  transfers between devices with their start and end apart: 4 -> 4, of which waited for: 4 -> 4; matrix products, arithmetic and copies ran while one was open for 7% -> 6% of each run, Pallas kernels for 0% -> 0%
where the time goes in v1:
time: 1450 us; the launch traced here: 1440 us
  waiting for transfers between devices  848 us (58%)
  matrix products  237 us (16%)
  local copies, waits for them, and re-layouts  192 us (13%)
  other arithmetic  128 us (9%)
  blocking collectives  24.2 us (2%)
  between operations  14.7 us (1%)
    psum x1, waiting for transfers between devices, body(): lax.psum(jnp.dot(hidden_act, w_down, preferred_element_type=jnp.float32)....  319 us
    all_gather x1, waiting for transfers between devices, summed_here(): parts = lax.all_gather(x, axis)  304 us
    psum x1, waiting for transfers between devices, body(): lax.psum(jnp.dot(head_flat, out_rows, preferred_element_type=jnp.float32)...  147 us
    psum x1, waiting for transfers between devices, body(): lax.psum(grad_w_qkv.astype(jnp.bfloat16), 'dp').astype(jnp.float32)  78 us
    dynamic_update_slice x8, local copies, waits for them, and re-layouts, body(): lax.map(lambda packed: attend_back(packed[0], packed[1], packed[2], packe...  56.6 us
    dot_general x4, matrix products, attend_back(): jnp.einsum('hqk,khd->qhd', grad_score, key_rows, preferred_element_type=j...  48.1 us
    dot_general x4, matrix products, attend_back(): jnp.einsum('hqk,qhd->khd', grad_score, queries, preferred_element_type=jn...  47.1 us
    unnamed x83, local copies, waits for them, and re-layouts  35.8 us
  transfers between devices with their start and end apart: 4, of which 4 were waited for; matrix products, arithmetic and copies ran while one was open for 6% of the time, Pallas kernels for 0%

profile of v1, /device:TPU:0, one launch (start us, length us, event | category | flops | bytes accessed | tf_op | source)
XLA Modules:
  0.0 1444.7 jit_solution(14087641368007954065)
XLA Ops:
  57.4 25.5 %while.26 = (s32[]{:T(128)}, bf16[4,577,4,64]{1,3,2,0:T(8,128)(2,1)}, f32[4,4,577]{2,1,0:T(4,128)S(1)}, bf16[4,577,4,64]{1,3,2,0:T(8,128)(2,1)}, bf16[4,577,4,64...) while((s32[]{:T(128)}, bf16[4,577,4,64]{1,3,2,0:T(8,128)(2,1)}, ...), condition=%wide.region_5.6_spmd, body=%wide.region_2.5_spmd.sunk | while | flops 353050112 | bytes 17370328 | solution.py:111
  124.2 146.7 %all-reduce.7.cloned.1.call-done = bf16[2308,1024]{1,0:T(8,128)(2,1)} async-done(((bf16[2308,1024]{1,0:T(8,128)(2,1)}), bf16[2308,1024]{1,0:T(8,128)(2,1)}) %all-reduce.7.cloned.1.call-update) | async-done | bytes 4726800 | tf_op jit(solution)/shard_map/psum | solution.py:117
  297.2 11.2 fusion.133
  317.4 10.2 convolution_convert_fusion.4
  335.8 304.3 %all-gather.4.cloned.1.call-done = bf16[4,2308,1024]{2,1,0:T(8,128)(2,1)} async-done(((bf16[1,2308,1024]{2,1,0:T(8,128)(2,1)}), bf16[4,2308,1024]{2,1,0:T(8,128)(2,1)}) %all-gather.4.cloned.1.call-update) | async-done | bytes 18907152 | tf_op jit(solution)/shard_map/all_gather | solution.py:11
  640.1 18.4 %fusion.128 = (bf16[1024]{0:T(1024)(128)(2,1)}, bf16[2308,1024]{1,0:T(8,128)(2,1)}) fusion(bf16[4,2308,1024]{2,1,0:T(8,128)(2,1)} %all-gather.4.cloned.1.call-done), kind=kLoop, calls=%fused_computation.144 | loop fusion | flops 16542720 | bytes 23635968 | tf_op jit(solution)/shard_map/reduce_sum | solution.py:31
  686.8 198.0 %while.27 = (s32[]{:T(128)}, f32[4,577,4,64]{1,3,2,0:T(8,128)}, bf16[4,577,4,64]{1,0,3,2:T(4,128)(2,1)}, f32[4,577,4,64]{1,3,2,0:T(8,128)}, bf16[4,577,4,64]{1,3...) while((s32[]{:T(128)}, f32[4,577,4,64]{1,3,2,0:T(8,128)}, ...), condition=%wide.region_15.16_spmd, body=%wide.region_13.15_spmd.sunk | while | flops 880270016 | bytes 90938144 | solution.py:158
  698.7 11.8 fusion.183
  710.5 12.0 fusion.182
  724.0 12.7 dynamic_update_slice.31
  748.1 11.8 fusion.183
  759.9 12.0 fusion.182
  773.4 12.7 dynamic_update_slice.31
  797.4 11.8 fusion.183
  809.2 12.0 fusion.182
  822.7 12.7 dynamic_update_slice.31
  846.8 11.8 fusion.183
  858.6 12.0 fusion.182
  872.1 12.7 dynamic_update_slice.31
  931.6 78.0 %all-reduce.9.cloned.1.call-done = (bf16[1024,3,4,64]{0,3,2,1:T(8,128)(2,1)}, bf16[4,64,1024]{2,1,0:T(8,128)(2,1)}, bf16[1024,1024]{1,0:T(8,128)(2,1)}, bf16[1024,1024]{1,0:T(8,128)(2,1)}) async-done(((bf16[1024,3,4,64]{0,3,2,1:T(8,128)(2,1)}, bf16[4,64,1024]{2,1,0:T(8,128)(2,1)}, bf16[1024,1024]{1,0:T(8,128)(2,1)}, bf16[1024,1024]{1,0:T(8,128)(2,1)}), (bf16[1024,3,4,64]{0,3,2,1:T(8,128)(2,1)}, ...) | async-done | bytes 6291472 | tf_op jit(solution)/shard_map/psum | solution.py:189
  1020.3 318.5 %all-reduce.11.cloned.1.call-done = (bf16[2308,1024]{1,0:T(8,128)(2,1)}, bf16[2308,1024]{1,0:T(8,128)(2,1)}) async-done(((bf16[2308,1024]{1,0:T(8,128)(2,1)}, bf16[2308,1024]{1,0:T(8,128)(2,1)}), (bf16[2308,1024]{1,0:T(8,128)(2,1)}, bf16[2308,1024]{1,0:T(8,128)(2,1)})) %all-reduce.11.cloned.1.call-update) | async-done | bytes 9453584 | tf_op jit(solution)/shard_map/psum | solution.py:126
  1350.4 24.2 %all-reduce = (bf16[1024]{0:T(1024)(128)(2,1)S(1)}, bf16[1024]{0:T(1024)(128)(2,1)S(1)}, bf16[2,4,64]{2,1,0:T(4,128)(2,1)S(1)}, bf16[1024]{0:T(1024)(128)(2,1)S(...) all-reduce(bf16[1024]{0:T(1024)(128)(2,1)S(1)} %get-tuple-element.2, ...), channel_id=1, replica_groups=mesh['dp'=8,'tensor'=4] {'dp'}, use_global_device_ids=true, to_apply=%region_20.21 | all-reduce | flops 7680 | bytes 30720 | tf_op jit(solution)/shard_map/psum | solution.py:187
  1402.3 13.3 fusion.94
  1424.2 13.5 copy.108
  (211 shorter events, 344.8 us)
Async XLA Ops:
  7.2 278.8 %copy-start = (bf16[1024,1024]{1,0:T(8,128)(2,1)S(1)}, bf16[1024,1024]{1,0:T(8,128)(2,1)}, u32[]{:S(2)}) copy-start(bf16[1024,1024]{1,0:T(8,128)(2,1)} %param.27) | copy-start | bytes 6291460
  7.2 8.6 copy-start.19
  7.2 8.6 copy-start.24
  7.2 263.8 %all-reduce.7.cloned.1.call-start = ((), (), s32[]{:S(2)}) async-start(), calls=%async_computation | async-start | bytes 9469952 | tf_op jit(solution)/shard_map/psum | solution.py:117
  11.7 8.5 copy-start.10
  82.9 12.5 copy-start.7
  95.4 544.7 %all-gather.4.cloned.1.call-start = ((), (), s32[]{:S(2)}) async-start(), calls=%async_computation.1 | async-start | bytes 23674880 | tf_op jit(solution)/shard_map/all_gather | solution.py:11
  115.7 155.2 %copy-start.25 = (f32[1024]{0:T(1024)S(1)}, f32[1024]{0:T(1024)}, u32[]{:S(2)}) copy-start(f32[1024]{0:T(1024)} %param.24) | copy-start | bytes 12292
  281.0 16.2 %slice-start.3 = ((s8[4734976]{0:T(1024)(128)(4,1)}), s8[4194304]{0:T(1024)(128)(4,1)S(1)}, s32[]{:S(2)}) async-start(s8[4734976]{0:T(1024)(128)(4,1)} %bitcast.174), calls=%async_computation.7 | async-start | bytes 8388608
  287.4 9.8 slice-start.4
  287.4 9.8 copy-start.29
  317.3 10.4 slice-start
  317.3 692.3 %all-reduce.9.cloned.1.call-start = ((), (), s32[]{:S(2)}) async-start(), calls=%async_computation.2 | async-start | bytes 12582912 | tf_op jit(solution)/shard_map/psum | solution.py:189
  317.4 10.2 slice-start.1
  317.4 10.2 slice-start.2
  317.4 10.2 copy-start.34
  658.5 9.3 copy-start.6
  906.6 9.6 copy-start.17
  906.6 432.3 %all-reduce.11.cloned.1.call-start = ((), (), s32[]{:S(2)}) async-start(), calls=%async_computation.3 | async-start | bytes 18939904 | tf_op jit(solution)/shard_map/psum | solution.py:126
  906.6 9.5 copy-start.18
  906.7 9.5 copy-start.30
  1017.8 324.1 %copy-start.20 = (f32[1024]{0:T(1024)S(1)}, f32[1024]{0:T(1024)}, u32[]{:S(2)}) copy-start(f32[1024]{0:T(1024)} %param.19) | copy-start | bytes 12292
  1342.0 37.4 %copy-start.27 = (f32[1024]{0:T(1024)S(1)}, f32[1024]{0:T(1024)}, u32[]{:S(2)}) copy-start(f32[1024]{0:T(1024)} %param.30) | copy-start | bytes 12292
  1415.6 22.1 %copy-start.1 = (bf16[1024,1024]{1,0:T(8,128)(2,1)S(1)}, bf16[1024,1024]{1,0:T(8,128)(2,1)}, u32[]{:S(2)}) copy-start(bf16[1024,1024]{1,0:T(8,128)(2,1)} %param.27) | copy-start | bytes 6291460
  (23 other events, 108.5 us)
Sparse Core Ops, SparseCore 0:
  95.5 175.3 all-reduce.6
  317.5 322.5 all-gather.3
  906.7 102.8 all-reduce.8
  1012.6 326.1 all-reduce.10
